TPU v7x, 32 devices: a whole 2x2x4 slice. The times are simulated.
32 devices in a mesh: dp: 8 (over y, x, core), tensor: 4 (over z).
Axes of the slice: x: 2, y: 2, z: 4, core: 2. Of those that a mesh axis runs over, the one named last changes fastest.
Arguments:
- tokens: bfloat16 [16384, 768], P('dp'), may hold values from -24 to 24
- lengths: int32 [8, 8], P('dp'), may hold values from 1 to 512, 2048 in all within a row
- w_qkv: bfloat16 [3, 768, 768], P(None, None, 'tensor'), may hold values from -0.21875 to 0.21875
- b_qv: bfloat16 [2, 768], P(None, 'tensor'), may hold values from -3 to 3
- w_out: bfloat16 [768, 768], P('tensor'), may hold values from -0.875 to 0.875
- b_out: bfloat16 [768], replicated, may hold values from -3 to 3
- ln1_gain: bfloat16 [768], replicated, may hold values from 0.099609375 to 1.8984375
- ln1_bias: bfloat16 [768], replicated, may hold values from -3 to 3
- w_up: bfloat16 [768, 3072], P(None, 'tensor'), may hold values from -0.21875 to 0.21875
- b_up: bfloat16 [3072], P('tensor'), may hold values from -3 to 3
- w_down: bfloat16 [3072, 768], P('tensor'), may hold values from -0.109375 to 0.109375
- b_down: bfloat16 [768], replicated, may hold values from -3 to 3
- ln2_gain: bfloat16 [768], replicated, may hold values from 0.099609375 to 1.8984375
- ln2_bias: bfloat16 [768], replicated, may hold values from -3 to 3
- cotangent: bfloat16 [16384, 768], P('dp'), may hold values from -24 to 24
Outputs:
- layer_out: bfloat16 [16384, 768], P(('dp', 'tensor'))
- input_grad: bfloat16 [16384, 768], P(('dp', 'tensor'))
- grad_qkv: float32 [3, 768, 768], P(None, 'dp', 'tensor')
- grad_qv_bias: float32 [2, 768], P(None, 'tensor')
- grad_out: float32 [768, 768], P('tensor', 'dp')
- grad_out_bias: float32 [768], P('dp')
- grad_norm1_gain: float32 [768], P('dp')
- grad_norm1_bias: float32 [768], P('dp')
- grad_up: float32 [768, 3072], P('dp', 'tensor')
- grad_up_bias: float32 [3072], P('tensor')
- grad_down: float32 [3072, 768], P('tensor', 'dp')
- grad_down_bias: float32 [768], P('dp')
- grad_norm2_gain: float32 [768], P('dp')
- grad_norm2_bias: float32 [768], P('dp')
Inputs may be any that keep to these rules, and one draw needn't show every extreme that they name: Each row holds 8 lengths that sum to 2048; the longest pair of every pack has exactly 512 tokens.
All inputs are finite; a program needn't handle non-finite values.
Results may differ from a plain program's by a relative error of at most 0.02.
Values may be sent and summed in bfloat16 or wider, within the bound.
A program may use at most 192 MiB of HBM per device.

v0:
```python
import jax
import jax.numpy as jnp
from jax import lax
from jax.sharding import PartitionSpec as P

HD = 64
MOST = 512
epsilon = 1e-05


def segment_ids(pair_lengths, count):
    pair_ends = jnp.cumsum(pair_lengths)
    positions = jnp.arange(count, dtype=jnp.int32)
    return jnp.sum((positions[:, None] >= pair_ends[None, :]).astype(jnp.int32), axis=1)


def norm_forward(values, gain, shift_bias):
    average = jnp.mean(values, axis=-1, keepdims=True)
    centred = values - average
    inv_spread = lax.rsqrt(jnp.mean(centred * centred, axis=-1, keepdims=True) + epsilon)
    normed = centred * inv_spread
    return (normed * gain + shift_bias, normed, inv_spread)


def norm_backward(upstream, normed, inv_spread, gain):
    scaled = upstream * gain
    adjusted = (
        scaled
        - jnp.mean(scaled, axis=-1, keepdims=True)
        - normed * jnp.mean(scaled * normed, axis=-1, keepdims=True)
    )
    return (adjusted * inv_spread, jnp.sum(upstream * normed, axis=0), jnp.sum(upstream, axis=0))


def gelu_exact(value):
    return jax.nn.gelu(value, approximate=False)


def per_device(
    tokens,
    lengths,
    w_qkv,
    b_qv,
    w_out,
    b_out,
    ln1_gain,
    ln1_bias,
    w_up,
    b_up,
    w_down,
    b_down,
    ln2_gain,
    ln2_bias,
    cotangent,
):
    rows = tokens.shape[0]
    local_width = w_out.shape[0]
    local_heads = local_width // HD
    blocks = rows // MOST
    window_rows = 3 * MOST
    factor = HD ** (-0.5)
    segment = segment_ids(lengths[0], rows)
    segment_pad = jnp.pad(segment, (MOST, MOST), constant_values=-1)
    projected = jnp.einsum("td,cde->cte", tokens, w_qkv, preferred_element_type=jnp.float32)
    bias_rows = jnp.stack([b_qv[0], jnp.zeros_like(b_qv[0]), b_qv[1]]).astype(jnp.float32)
    qkv_low = (projected + bias_rows[:, None, :]).astype(jnp.bfloat16)
    padded = jnp.pad(qkv_low[1:], ((0, 0), (MOST, MOST), (0, 0)))

    def block_scores(block_index):
        offset = block_index * MOST
        queries = lax.dynamic_slice_in_dim(qkv_low[0], offset, MOST, 0).reshape(
            MOST, local_heads, HD
        )
        window = lax.dynamic_slice_in_dim(padded, offset, window_rows, 1).reshape(
            2, window_rows, local_heads, HD
        )
        query_segment = lax.dynamic_slice_in_dim(segment, offset, MOST, 0)
        key_segment = lax.dynamic_slice_in_dim(segment_pad, offset, window_rows, 0)
        allowed = query_segment[:, None] == key_segment[None, :]
        products = (
            jnp.einsum("qhd,khd->hqk", queries, window[0], preferred_element_type=jnp.float32)
            * factor
        )
        return (jnp.where(allowed[None], products, -1e30), queries, window)

    def forward_block(block_index):
        scores, queries, window = block_scores(block_index)
        row_top = jnp.max(scores, axis=-1, keepdims=True)
        row_total = jnp.sum(jnp.exp(scores - row_top), axis=-1, keepdims=True)
        log_total = row_top + jnp.log(row_total)
        soft_weights = jnp.exp(scores - log_total).astype(jnp.bfloat16)
        context = jnp.einsum(
            "hqk,khd->qhd", soft_weights, window[1], preferred_element_type=jnp.float32
        )
        return (context.reshape(MOST, local_width).astype(jnp.bfloat16), log_total[..., 0])

    contexts, log_totals = lax.map(forward_block, jnp.arange(blocks, dtype=jnp.int32))
    context = contexts.reshape(rows, local_width)
    attended = lax.psum(
        jnp.dot(context, w_out, preferred_element_type=jnp.float32).astype(jnp.bfloat16), "tensor"
    ).astype(jnp.float32)
    mixed_one = tokens.astype(jnp.float32) + attended + b_out.astype(jnp.float32)
    gain_one = ln1_gain.astype(jnp.float32)
    hidden_one, normed_one, spread_one = norm_forward(
        mixed_one, gain_one, ln1_bias.astype(jnp.float32)
    )
    hidden_low = hidden_one.astype(jnp.bfloat16)
    pre_act = jnp.dot(hidden_low, w_up, preferred_element_type=jnp.float32) + b_up.astype(
        jnp.float32
    )
    activated = gelu_exact(pre_act).astype(jnp.bfloat16)
    fed = lax.psum(
        jnp.dot(activated, w_down, preferred_element_type=jnp.float32).astype(jnp.bfloat16),
        "tensor",
    ).astype(jnp.float32)
    mixed_two = hidden_one + fed + b_down.astype(jnp.float32)
    gain_two = ln2_gain.astype(jnp.float32)
    output_full, normed_two, spread_two = norm_forward(
        mixed_two, gain_two, ln2_bias.astype(jnp.float32)
    )
    share = rows // lax.axis_size("tensor")
    own_start = lax.axis_index("tensor") * share
    layer_out = lax.dynamic_slice_in_dim(output_full, own_start, share, 0).astype(jnp.bfloat16)
    upstream = cotangent.astype(jnp.float32)
    grad_mixed_two, grad_gain_two, grad_bias_two = norm_backward(
        upstream, normed_two, spread_two, gain_two
    )
    grad_fed = grad_mixed_two.astype(jnp.bfloat16)
    grad_down_t = jnp.einsum("td,tf->df", grad_fed, activated, preferred_element_type=jnp.float32)
    grad_act = jnp.einsum("td,fd->tf", grad_fed, w_down, preferred_element_type=jnp.float32)
    act_pull = jax.vjp(gelu_exact, pre_act)[1]
    grad_pre = act_pull(grad_act)[0].astype(jnp.bfloat16)
    grad_up_local = jnp.einsum(
        "td,tf->df", hidden_low, grad_pre, preferred_element_type=jnp.float32
    )
    up_bias_sum = jnp.sum(grad_pre.astype(jnp.float32), axis=0)
    partial_hidden = jnp.einsum("tf,df->td", grad_pre, w_up, preferred_element_type=jnp.float32)
    grad_hidden_one = (
        lax.psum(partial_hidden.astype(jnp.bfloat16), "tensor").astype(jnp.float32) + grad_mixed_two
    )
    grad_mixed_one, grad_gain_one, grad_bias_one = norm_backward(
        grad_hidden_one, normed_one, spread_one, gain_one
    )
    sum_mixed_one = jnp.sum(grad_mixed_one, axis=0)
    grad_attended = grad_mixed_one.astype(jnp.bfloat16)
    own_mixed_one = lax.dynamic_slice_in_dim(grad_mixed_one, own_start, share, 0)
    grad_out_t = jnp.einsum("td,tc->dc", grad_attended, context, preferred_element_type=jnp.float32)
    grad_context = jnp.einsum(
        "td,cd->tc", grad_attended, w_out, preferred_element_type=jnp.float32
    ).astype(jnp.bfloat16)

    def backward_block(gathered_grads, block_index):
        offset = block_index * MOST
        scores, queries, window = block_scores(block_index)
        soft_weights = jnp.exp(scores - log_totals[block_index][..., None])
        upstream_block = lax.dynamic_slice_in_dim(grad_context, offset, MOST, 0).reshape(
            MOST, local_heads, HD
        )
        grad_values = jnp.einsum(
            "hqk,qhd->khd",
            soft_weights.astype(jnp.bfloat16),
            upstream_block,
            preferred_element_type=jnp.float32,
        )
        grad_weights = jnp.einsum(
            "qhd,khd->hqk", upstream_block, window[1], preferred_element_type=jnp.float32
        )
        row_shift = jnp.sum(grad_weights * soft_weights, axis=-1, keepdims=True)
        grad_scores = (soft_weights * (grad_weights - row_shift)).astype(jnp.bfloat16)
        grad_queries = (
            jnp.einsum("hqk,khd->qhd", grad_scores, window[0], preferred_element_type=jnp.float32)
            * factor
        )
        grad_keys = (
            jnp.einsum("hqk,qhd->khd", grad_scores, queries, preferred_element_type=jnp.float32)
            * factor
        )
        update = jnp.stack(
            [
                grad_keys.reshape(window_rows, local_width),
                grad_values.reshape(window_rows, local_width),
            ]
        )
        current = lax.dynamic_slice_in_dim(gathered_grads, offset, window_rows, 1)
        gathered_grads = lax.dynamic_update_slice_in_dim(
            gathered_grads, current + update, offset, 1
        )
        return (gathered_grads, grad_queries.reshape(MOST, local_width))

    start_grads = jnp.zeros((2, rows + 2 * MOST, local_width), jnp.float32)
    key_value_grads, query_grads = lax.scan(
        backward_block, start_grads, jnp.arange(blocks, dtype=jnp.int32)
    )
    key_value_grads = key_value_grads[:, MOST : MOST + rows]
    grad_qkv_low = jnp.stack(
        [query_grads.reshape(rows, local_width), key_value_grads[0], key_value_grads[1]]
    ).astype(jnp.bfloat16)
    grad_qkv_t = jnp.einsum("td,cte->dce", tokens, grad_qkv_low, preferred_element_type=jnp.float32)
    qkv_bias_sums = jnp.sum(grad_qkv_low.astype(jnp.float32), axis=1)
    partial_input = jnp.einsum(
        "cte,cde->td", grad_qkv_low, w_qkv, preferred_element_type=jnp.float32
    )
    input_share = lax.psum_scatter(
        partial_input.astype(jnp.bfloat16), "tensor", scatter_dimension=0, tiled=True
    ).astype(jnp.float32)
    input_grad = (input_share + own_mixed_one).astype(jnp.bfloat16)
    bias_grads, up_bias_grad = lax.psum(
        (jnp.stack([qkv_bias_sums[0], qkv_bias_sums[2]]), up_bias_sum), "dp"
    )
    small_stack = jnp.stack(
        [
            sum_mixed_one,
            grad_gain_one,
            grad_bias_one,
            jnp.sum(grad_mixed_two, axis=0),
            grad_gain_two,
            grad_bias_two,
        ],
        axis=1,
    )
    qkv_share, out_share, small_share, up_share, down_share = (
        lax.psum_scatter(grad_qkv_t, "dp", scatter_dimension=0, tiled=True),
        lax.psum_scatter(grad_out_t, "dp", scatter_dimension=0, tiled=True),
        lax.psum_scatter(small_stack, "dp", scatter_dimension=0, tiled=True),
        lax.psum_scatter(grad_up_local, "dp", scatter_dimension=0, tiled=True),
        lax.psum_scatter(grad_down_t, "dp", scatter_dimension=0, tiled=True),
    )
    return (
        layer_out,
        input_grad,
        jnp.transpose(qkv_share, (1, 0, 2)),
        bias_grads,
        out_share.T,
        small_share[:, 0],
        small_share[:, 1],
        small_share[:, 2],
        up_share,
        up_bias_grad,
        down_share.T,
        small_share[:, 3],
        small_share[:, 4],
        small_share[:, 5],
    )


def solution(mesh):
    return jax.shard_map(
        per_device,
        mesh=mesh,
        in_specs=(
            P("dp", None),
            P("dp", None),
            P(None, None, "tensor"),
            P(None, "tensor"),
            P("tensor", None),
            P(),
            P(),
            P(),
            P(None, "tensor"),
            P("tensor"),
            P("tensor", None),
            P(),
            P(),
            P(),
            P("dp", None),
        ),
        out_specs=(
            P(("dp", "tensor"), None),
            P(("dp", "tensor"), None),
            P(None, "dp", "tensor"),
            P(None, "tensor"),
            P("tensor", "dp"),
            P("dp"),
            P("dp"),
            P("dp"),
            P("dp", "tensor"),
            P("tensor"),
            P("tensor", "dp"),
            P("dp"),
            P("dp"),
            P("dp"),
        ),
        check_vma=False,
    )
```

profile of v0, /device:TPU:0, one launch (start us, length us, event | category | flops | bytes accessed | tf_op | source)
XLA Modules:
  0.0 893.2 jit_solution(6782802428937616471)
XLA Ops:
  9.8 4.2 fusion.30
  15.4 51.2 %while.24 = (s32[]{:T(128)}, bf16[4,512,192]{1,2,0:T(8,128)(2,1)}, f32[4,3,512]{2,1,0:T(4,128)}, s32[4]{0:T(128)S(1)}, bf16[2,3072,192]{1,2,0:T(8,128)(2,1)S(1)}...) while((s32[]{:T(128)}, bf16[4,512,192]{1,2,0:T(8,128)(2,1)}, ...), condition=%wide.region_5.6_spmd, body=%wide.region_2.5_spmd.sunk | while | flops 630815232 | bytes 37824776 | solution.py:97
  21.3 2.8 exponential_reduce_fusion.2
  34.1 2.8 exponential_reduce_fusion.2
  46.9 2.8 exponential_reduce_fusion.2
  59.7 2.8 exponential_reduce_fusion.2
  68.7 3.7 convolution_convert_fusion.2
  77.5 118.8 %all-reduce.7.cloned.1.call-done = bf16[2048,768]{1,0:T(8,128)(2,1)} async-done(((bf16[2048,768]{1,0:T(8,128)(2,1)}), bf16[2048,768]{1,0:T(8,128)(2,1)}) %all-reduce.7.cloned.1.call-update) | async-done | bytes 3145744 | tf_op jit(solution)/shard_map/psum | solution.py:99
  196.3 4.1 fusion.23
  202.8 18.6 %multiply_convert_fusion.1 = (bf16[2048,768]{1,0:T(8,128)(2,1)S(1)}, f32[2048,768]{1,0:T(8,128)}, f32[2048,768]{1,0:T(8,128)}) fusion(f32[768]{0:T(1024)S(1)} %copy-done.42, bf16[768,768]{1,0:T(8,128)(2,1)S(1)} %copy-done, f32[768]{0:T(1024)S(1)} %copy-done.38, f32[768]{0:T(1024)S(1)} %copy-done.34, f32[2048]{0:T(1024)S(1)} %add_rsqrt_fusion.1, ...), kind=kOutput, calls=%fused_computation.53 | convolution fusion | flops 2533883904 | bytes 23228416 | tf_op jit(solution)/shard_map/dot_general | solution.py:108
  223.1 4.0 convolution_convert_fusion.1
  229.9 117.4 %all-reduce.9.cloned.1.call-done = bf16[2048,768]{1,0:T(8,128)(2,1)} async-done(((bf16[2048,768]{1,0:T(8,128)(2,1)}), bf16[2048,768]{1,0:T(8,128)(2,1)}) %all-reduce.9.cloned.1.call-update) | async-done | bytes 3145744 | tf_op jit(solution)/shard_map/psum | solution.py:112
  347.3 6.5 fusion.48
  353.9 3.9 multiply_reduce_fusion.3
  357.8 6.5 fusion.16
  367.0 10.4 %convert_reduce_fusion.1 = (f32[768]{0:T(1024)}, bf16[2048,768]{1,0:T(8,128)(2,1)S(1)}) fusion(f32[2048,768]{1,0:T(8,128)} %get-tuple-element.223, bf16[768,768]{1,0:T(8,128)(2,1)S(1)} %copy-done.45, f32[2048,768]{1,0:T(8,128)S(1)} %fusion.13, f32[2048,768]{1,0:T(8,128)} %get-tuple-element.242, f32[768]{0:T(1024)S(1)} %copy-done.43), kind=kOutput, calls=%fused_computation.45 | convolution fusion | flops 2444229888 | bytes 23205888 | tf_op jit(solution)/shard_map/td,fd->tf/dot_general | solution.py:130
  379.0 4.0 convolution_convert_fusion
  384.7 118.6 %all-reduce.11.cloned.1.call-done = bf16[2048,768]{1,0:T(8,128)(2,1)} async-done(((bf16[2048,768]{1,0:T(8,128)(2,1)}), bf16[2048,768]{1,0:T(8,128)(2,1)}) %all-reduce.11.cloned.1.call-update) | async-done | bytes 3145744 | tf_op jit(solution)/shard_map/psum | solution.py:139
  503.3 7.9 multiply_reduce_fusion.1
  511.6 5.7 fusion.52
  523.0 4.8 convolution_convert_fusion.3
  528.2 2.8 broadcast_in_dim.42
  531.0 148.0 %while.25 = (s32[]{:T(128)}, f32[2,3072,192]{1,2,0:T(8,128)}, bf16[4,512,192]{1,2,0:T(8,128)(2,1)}, s32[4]{0:T(128)S(1)}, bf16[3,2048,192]{1,2,0:T(8,128)(2,1)},...) while((s32[]{:T(128)}, f32[2,3072,192]{1,2,0:T(8,128)}, ...), condition=%wide.region_19.20_spmd, body=%wide.region_17.19_spmd.sunk | while | flops 1533639168 | bytes 149576176 | solution.py:191
  542.7 5.6 multiply_reduce_fusion.7
  548.3 9.4 %multiply_convert_fusion.3 = bf16[3,512,1536]{2,1,0:T(8,128)(2,1)} fusion(f32[3,512,1536]{2,1,0:T(8,128)} %copy-done.2, f32[3,512,1536]{2,1,0:T(8,128)} %get-tuple-element.375, f32[3,512]{1,0:T(4,128)S(1)} %get-tuple-element.376), kind=kLoop, calls=%fused_computation.16.clone.1 | loop fusion | flops 7077888 | bytes 23599104 | tf_op jit(solution)/shard_map/while/body/eval_jaxpr/convert_element_type | solution.py:169
  557.8 4.2 convolution_multiply_fusion.5
  564.5 3.5 fusion.116
  579.8 5.6 multiply_reduce_fusion.7
  585.4 9.5 %multiply_convert_fusion.3 = bf16[3,512,1536]{2,1,0:T(8,128)(2,1)} fusion(f32[3,512,1536]{2,1,0:T(8,128)} %copy-done.2, f32[3,512,1536]{2,1,0:T(8,128)} %get-tuple-element.375, f32[3,512]{1,0:T(4,128)S(1)} %get-tuple-element.376), kind=kLoop, calls=%fused_computation.16.clone.1 | loop fusion | flops 7077888 | bytes 23599104 | tf_op jit(solution)/shard_map/while/body/eval_jaxpr/convert_element_type | solution.py:169
  594.9 4.2 convolution_multiply_fusion.5
  601.7 3.5 fusion.116
  616.9 5.5 multiply_reduce_fusion.7
  622.4 9.4 %multiply_convert_fusion.3 = bf16[3,512,1536]{2,1,0:T(8,128)(2,1)} fusion(f32[3,512,1536]{2,1,0:T(8,128)} %copy-done.2, f32[3,512,1536]{2,1,0:T(8,128)} %get-tuple-element.375, f32[3,512]{1,0:T(4,128)S(1)} %get-tuple-element.376), kind=kLoop, calls=%fused_computation.16.clone.1 | loop fusion | flops 7077888 | bytes 23599104 | tf_op jit(solution)/shard_map/while/body/eval_jaxpr/convert_element_type | solution.py:169
  631.8 4.2 convolution_multiply_fusion.5
  638.6 3.5 fusion.116
  653.8 5.5 multiply_reduce_fusion.7
  659.4 9.4 %multiply_convert_fusion.3 = bf16[3,512,1536]{2,1,0:T(8,128)(2,1)} fusion(f32[3,512,1536]{2,1,0:T(8,128)} %copy-done.2, f32[3,512,1536]{2,1,0:T(8,128)} %get-tuple-element.375, f32[3,512]{1,0:T(4,128)S(1)} %get-tuple-element.376), kind=kLoop, calls=%fused_computation.16.clone.1 | loop fusion | flops 7077888 | bytes 23599104 | tf_op jit(solution)/shard_map/while/body/eval_jaxpr/convert_element_type | solution.py:169
  668.8 4.2 convolution_multiply_fusion.5
  675.5 3.5 fusion.116
  683.5 5.2 fusion.24
  688.6 2.8 copy.48
  691.8 4.0 bitcast_convert_fusion
  696.0 8.2 fusion.38
  704.3 8.6 fusion.44
  716.4 14.7 %all-reduce.2 = (f32[2,192]{1,0:T(2,128)}, f32[768]{0:T(1024)}) all-reduce(f32[2,192]{1,0:T(2,128)S(1)} %pad_maximum_fusion.3, f32[768]{0:T(1024)S(1)} %copy-done.41), channel_id=1, replica_groups=mesh['dp'=8,'tensor'=4] {'dp'}, use_global_device_ids=true, to_apply=%region_23.24 | all-reduce | flops 1152 | bytes 9216 | tf_op jit(solution)/shard_map/psum | solution.py:207
  739.4 54.3 %reduce-scatter.11.cloned.1.call-done = bf16[512,768]{1,0:T(8,128)(2,1)} async-done(((bf16[2048,768]{1,0:T(8,128)(2,1)}), bf16[512,768]{1,0:T(8,128)(2,1)}) %reduce-scatter.11.cloned.1.call-update) | async-done | bytes 786448 | tf_op jit(solution)/shard_map/reduce_scatter | solution.py:203
  796.3 43.5 %reduce-scatter.17.cloned.1.call-done = f32[96,768]{1,0:T(8,128)} async-done(((f32[768,768]{1,0:T(8,128)}), f32[96,768]{1,0:T(8,128)}) %reduce-scatter.17.cloned.1.call-update) | async-done | bytes 294928 | tf_op jit(solution)/shard_map/reduce_scatter | solution.py:226
  839.9 46.3 %reduce-scatter.15.cloned.1.call-done = f32[96,768]{1,0:T(8,128)} async-done(((f32[768,768]{1,0:T(8,128)}), f32[96,768]{1,0:T(8,128)}) %reduce-scatter.15.cloned.1.call-update) | async-done | bytes 294928 | tf_op jit(solution)/shard_map/reduce_scatter | solution.py:225
  (306 shorter events, 133.2 us)
Async XLA Ops:
  7.2 195.6 %copy-start = (bf16[768,768]{1,0:T(8,128)(2,1)S(1)}, bf16[768,768]{1,0:T(8,128)(2,1)}, u32[]{:S(2)}) copy-start(bf16[768,768]{1,0:T(8,128)(2,1)} %param.27) | copy-start | bytes 3538948
  7.2 189.1 %all-reduce.7.cloned.1.call-start = ((), (), s32[]{:S(2)}) async-start(), calls=%async_computation.6 | async-start | bytes 6291456 | tf_op jit(solution)/shard_map/psum | solution.py:99
  72.4 274.9 %all-reduce.9.cloned.1.call-start = ((), (), s32[]{:S(2)}) async-start(), calls=%async_computation.7 | async-start | bytes 6291456 | tf_op jit(solution)/shard_map/psum | solution.py:112
  73.6 437.6 %copy-start.33 = (f32[768]{0:T(1024)}, f32[768]{0:T(1024)S(1)}, u32[]{:S(2)}) copy-start(f32[768]{0:T(1024)S(1)} %convert_element_type.132) | copy-start | bytes 9220
  196.3 6.5 copy-start.34
  196.3 6.5 copy-start.38
  196.3 6.5 copy-start.42
  201.0 20.5 %copy-start.25 = (f32[2048]{0:T(1024)}, f32[2048]{0:T(1024)S(1)}, u32[]{:S(2)}) copy-start(f32[2048]{0:T(1024)S(1)} %broadcast_multiply_fusion.5) | copy-start | bytes 24580
  202.8 18.6 %copy-start.29 = (f32[2048]{0:T(1024)}, f32[2048]{0:T(1024)S(1)}, u32[]{:S(2)}) copy-start(f32[2048]{0:T(1024)S(1)} %add_rsqrt_fusion.1) | copy-start | bytes 24580
  202.8 20.2 %copy-start.44 = (bf16[768,768]{1,0:T(8,128)(2,1)S(1)}, bf16[768,768]{1,0:T(8,128)(2,1)}, u32[]{:S(2)}) copy-start(bf16[768,768]{1,0:T(8,128)(2,1)} %param.29) | copy-start | bytes 3538948
  227.1 276.2 %all-reduce.11.cloned.1.call-start = ((), (), s32[]{:S(2)}) async-start(), calls=%async_computation.8 | async-start | bytes 6291456 | tf_op jit(solution)/shard_map/psum | solution.py:139
  347.3 6.6 copy-start.5
  347.3 6.6 copy-start.8
  347.3 6.6 copy-start.15
  347.3 6.6 copy-start.26
  347.3 6.6 copy-start.30
  347.3 6.6 copy-start.35
  347.3 6.6 copy-start.39
  347.3 6.6 copy-start.40
  367.0 10.4 %copy-start.10 = (f32[2048,768]{1,0:T(8,128)}, f32[2048,768]{1,0:T(8,128)S(1)}, u32[]{:S(2)}) copy-start(f32[2048,768]{1,0:T(8,128)S(1)} %fusion.13) | copy-start | bytes 18874372
  383.1 348.0 %reduce-scatter.21.cloned.1.call-start = ((), (), s32[]{:S(2)}) async-start(), calls=%async_computation.14 | async-start | bytes 442368
  384.7 126.5 %copy-start.27 = (f32[2048]{0:T(1024)S(1)}, f32[2048]{0:T(1024)}, u32[]{:S(2)}) copy-start(f32[2048]{0:T(1024)} %copy-done.25) | copy-start | bytes 24580
  384.7 126.5 %copy-start.31 = (f32[2048]{0:T(1024)S(1)}, f32[2048]{0:T(1024)}, u32[]{:S(2)}) copy-start(f32[2048]{0:T(1024)} %copy-done.29) | copy-start | bytes 24580
  384.7 126.5 %copy-start.36 = (f32[768]{0:T(1024)S(1)}, f32[768]{0:T(1024)}, u32[]{:S(2)}) copy-start(f32[768]{0:T(1024)} %convert_element_type.133) | copy-start | bytes 9220
  503.3 8.0 copy-start.6
  503.3 8.0 copy-start.9
  503.3 8.3 copy-start.18
  511.6 8.4 copy-start.20
  523.0 212.8 %reduce-scatter.13.cloned.1.call-start = ((), (), s32[]{:S(2)}) async-start(), calls=%async_computation.10 | async-start | bytes 884736 | tf_op jit(solution)/shard_map/reduce_scatter | solution.py:223
  527.9 209.6 %reduce-scatter.19.cloned.1.call-start = ((), (), s32[]{:S(2)}) async-start(), calls=%async_computation.13 | async-start | bytes 2211840
  531.0 10.8 %copy-start.23 = (s32[3072]{0:T(1024)}, s32[3072]{0:T(1024)S(1)}, u32[]{:S(2)}) copy-start(s32[3072]{0:T(1024)S(1)} %get-tuple-element.459) | copy-start | bytes 36868 | tf_op jit(solution)/shard_map/while
  541.8 6.5 copy-start.2
  562.0 6.1 copy-start.24
  568.0 10.8 %copy-start.23 = (s32[3072]{0:T(1024)}, s32[3072]{0:T(1024)S(1)}, u32[]{:S(2)}) copy-start(s32[3072]{0:T(1024)S(1)} %get-tuple-element.459) | copy-start | bytes 36868 | tf_op jit(solution)/shard_map/while
  578.9 6.6 copy-start.2
  605.1 10.8 %copy-start.23 = (s32[3072]{0:T(1024)}, s32[3072]{0:T(1024)S(1)}, u32[]{:S(2)}) copy-start(s32[3072]{0:T(1024)S(1)} %get-tuple-element.459) | copy-start | bytes 36868 | tf_op jit(solution)/shard_map/while
  615.9 6.5 copy-start.2
  636.0 6.0 copy-start.24
  642.1 10.8 %copy-start.23 = (s32[3072]{0:T(1024)}, s32[3072]{0:T(1024)S(1)}, u32[]{:S(2)}) copy-start(s32[3072]{0:T(1024)S(1)} %get-tuple-element.459) | copy-start | bytes 36868 | tf_op jit(solution)/shard_map/while
  652.9 6.5 copy-start.2
  673.0 6.0 copy-start.24
  683.4 8.4 copy-start.46
  691.5 102.2 %reduce-scatter.11.cloned.1.call-start = ((), (), s32[]{:S(2)}) async-start(), calls=%async_computation.9 | async-start | bytes 3932160 | tf_op jit(solution)/shard_map/reduce_scatter | solution.py:203
  695.9 8.4 copy-start.28
  695.9 8.4 copy-start.32
  695.9 144.0 %reduce-scatter.17.cloned.1.call-start = ((), (), s32[]{:S(2)}) async-start(), calls=%async_computation.12 | async-start | bytes 2654208 | tf_op jit(solution)/shard_map/reduce_scatter | solution.py:226
  704.2 182.0 %reduce-scatter.15.cloned.1.call-start = ((), (), s32[]{:S(2)}) async-start(), calls=%async_computation.11 | async-start | bytes 2654208 | tf_op jit(solution)/shard_map/reduce_scatter | solution.py:225
  704.3 181.9 %copy-start.1 = (bf16[768,768]{1,0:T(8,128)(2,1)S(1)}, bf16[768,768]{1,0:T(8,128)(2,1)}, u32[]{:S(2)}) copy-start(bf16[768,768]{1,0:T(8,128)(2,1)} %param.27) | copy-start | bytes 3538948
  (27 other events, 71.0 us)
Sparse Core Ops, SparseCore 0:
  72.5 123.7 all-reduce.6
  227.2 120.0 all-reduce.8
  383.2 120.0 all-reduce.10
  523.1 32.8 reduce-scatter.20
  559.0 34.9 reduce-scatter.12
  691.6 39.2 reduce-scatter.18
  733.2 60.4 reduce-scatter.10
  797.6 42.2 reduce-scatter.16
  843.8 42.3 reduce-scatter.14
where the time goes:
time: 902 us; the launch traced here: 893 us
  waiting for transfers between devices  499 us (55%)
  matrix products  156 us (17%)
  other arithmetic  122 us (14%)
  local copies, waits for them, and re-layouts  70.1 us (8%)
  between operations  15 us (2%)
  blocking collectives  14.7 us (2%)
  loops' own time  13.6 us (2%)
    psum x1, waiting for transfers between devices, per_device(): lax.psum(jnp.dot(context, w_out, preferred_element_type=jnp.float32).asty...  119 us
    psum x1, waiting for transfers between devices, per_device(): lax.psum(partial_hidden.astype(jnp.bfloat16), 'tensor').astype(jnp.float32)  119 us
    psum x1, waiting for transfers between devices, per_device(): lax.psum(jnp.dot(activated, w_down, preferred_element_type=jnp.float32).a...  117 us
    reduce_scatter x1, waiting for transfers between devices, per_device(): lax.psum_scatter(partial_input.astype(jnp.bfloat16), 'tensor', scatter_di...  54.3 us
    reduce_scatter x1, waiting for transfers between devices, per_device(): lax.psum_scatter(grad_up_local, 'dp', scatter_dimension=0, tiled=True)  46.3 us
    reduce_scatter x1, waiting for transfers between devices, per_device(): lax.psum_scatter(grad_down_t, 'dp', scatter_dimension=0, tiled=True)  43.5 us
    convert_element_type x4, other arithmetic, backward_block(): (soft_weights * (grad_weights - row_shift)).astype(jnp.bfloat16)  37.7 us
    dot_general x4, matrix products, backward_block(): jnp.einsum('qhd,khd->hqk', upstream_block, window[1], preferred_element_t...  22.2 us
  transfers between devices with their start and end apart: 9, of which 6 were waited for; matrix products, arithmetic and copies ran while one was open for 22% of the time, Pallas kernels for 0%

commit v1 on v0

--- a/solution.py
+++ b/solution.py
@@ -96,8 +96,12 @@
 
     contexts, log_totals = lax.map(forward_block, jnp.arange(blocks, dtype=jnp.int32))
     context = contexts.reshape(rows, local_width)
-    attended = lax.psum(
-        jnp.dot(context, w_out, preferred_element_type=jnp.float32).astype(jnp.bfloat16), "tensor"
+    attended = jnp.sum(
+        lax.all_gather(
+            jnp.dot(context, w_out, preferred_element_type=jnp.float32).astype(jnp.bfloat16),
+            "tensor",
+        ),
+        axis=0,
     ).astype(jnp.float32)
     mixed_one = tokens.astype(jnp.float32) + attended + b_out.astype(jnp.float32)
     gain_one = ln1_gain.astype(jnp.float32)

time: 902 us -> 1010 us (1.12)
  waiting for transfers between devices: 499 us -> 596 us
    all_gather x0 -> x1, waiting for transfers between devices: none -> 216 us  [per_device(): lax.all_gather(jnp.dot(context, w_out, preferred_element_type=jnp.float32...]
    psum x1 -> x0, waiting for transfers between devices: 119 us -> none  [per_device(): lax.psum(jnp.dot(context, w_out, preferred_element_type=jnp.float32).asty...]
  transfers between devices with their start and end apart: 9 -> 9, of which waited for: 6 -> 6; matrix products, arithmetic and copies ran while one was open for 22% -> 20% of each run, Pallas kernels for 0% -> 0%
where the time goes in v1:
time: 1010 us; the launch traced here: 998 us
  waiting for transfers between devices  596 us (59%)
  matrix products  156 us (15%)
  other arithmetic  131 us (13%)
  local copies, waits for them, and re-layouts  70.9 us (7%)
  blocking collectives  14.6 us (1%)
  between operations  14.6 us (1%)
  loops' own time  13.6 us (1%)
    all_gather x1, waiting for transfers between devices, per_device(): lax.all_gather(jnp.dot(context, w_out, preferred_element_type=jnp.float32...  216 us
    psum x1, waiting for transfers between devices, per_device(): lax.psum(partial_hidden.astype(jnp.bfloat16), 'tensor').astype(jnp.float32)  119 us
    psum x1, waiting for transfers between devices, per_device(): lax.psum(jnp.dot(activated, w_down, preferred_element_type=jnp.float32).a...  117 us
    reduce_scatter x1, waiting for transfers between devices, per_device(): lax.psum_scatter(partial_input.astype(jnp.bfloat16), 'tensor', scatter_di...  54.5 us
    reduce_scatter x1, waiting for transfers between devices, per_device(): lax.psum_scatter(grad_up_local, 'dp', scatter_dimension=0, tiled=True)  46.3 us
    reduce_scatter x1, waiting for transfers between devices, per_device(): lax.psum_scatter(grad_down_t, 'dp', scatter_dimension=0, tiled=True)  43.6 us
    convert_element_type x4, other arithmetic, backward_block(): (soft_weights * (grad_weights - row_shift)).astype(jnp.bfloat16)  37.7 us
    dot_general x4, matrix products, backward_block(): jnp.einsum('qhd,khd->hqk', upstream_block, window[1], preferred_element_t...  22.2 us
  transfers between devices with their start and end apart: 9, of which 6 were waited for; matrix products, arithmetic and copies ran while one was open for 20% of the time, Pallas kernels for 0%

profile of v1, /device:TPU:0, one launch (start us, length us, event | category | flops | bytes accessed | tf_op | source)
XLA Modules:
  0.0 998.3 jit_solution(14041933590947355672)
XLA Ops:
  9.8 4.2 fusion.30
  15.4 51.2 %while.24 = (s32[]{:T(128)}, bf16[4,512,192]{1,2,0:T(8,128)(2,1)}, f32[4,3,512]{2,1,0:T(4,128)}, s32[4]{0:T(128)S(1)}, bf16[2,3072,192]{1,2,0:T(8,128)(2,1)S(1)}...) while((s32[]{:T(128)}, bf16[4,512,192]{1,2,0:T(8,128)(2,1)}, ...), condition=%wide.region_5.6_spmd, body=%wide.region_2.5_spmd.sunk | while | flops 630815232 | bytes 37824776 | solution.py:97
  21.3 2.8 exponential_reduce_fusion.2
  34.1 2.8 exponential_reduce_fusion.2
  46.9 2.8 exponential_reduce_fusion.2
  59.7 2.8 exponential_reduce_fusion.2
  68.7 3.7 convolution_convert_fusion.2
  77.1 216.3 %all-gather.3.cloned.1.call-done = bf16[8192,768]{1,0:T(8,128)(2,1)} async-done(((bf16[2048,768]{1,0:T(8,128)(2,1)}), bf16[8192,768]{1,0:T(8,128)(2,1)}) %all-gather.3.cloned.1.call-update) | async-done | bytes 12582928 | tf_op jit(solution)/shard_map/all_gather | solution.py:100
  293.4 8.9 reduce_sum.184
  302.4 4.1 fusion.23
  308.9 18.6 %multiply_convert_fusion.1 = (bf16[2048,768]{1,0:T(8,128)(2,1)S(1)}, f32[2048,768]{1,0:T(8,128)}, f32[2048,768]{1,0:T(8,128)}) fusion(f32[768]{0:T(1024)S(1)} %copy-done.42, bf16[768,768]{1,0:T(8,128)(2,1)S(1)} %copy-done, f32[768]{0:T(1024)S(1)} %copy-done.38, f32[768]{0:T(1024)S(1)} %copy-done.34, f32[2048]{0:T(1024)S(1)} %add_rsqrt_fusion.1, ...), kind=kOutput, calls=%fused_computation.53 | convolution fusion | flops 2533883904 | bytes 23228416 | tf_op jit(solution)/shard_map/dot_general | solution.py:112
  329.2 4.0 convolution_convert_fusion.1
  336.0 116.6 %all-reduce.6.cloned.1.call-done = bf16[2048,768]{1,0:T(8,128)(2,1)} async-done(((bf16[2048,768]{1,0:T(8,128)(2,1)}), bf16[2048,768]{1,0:T(8,128)(2,1)}) %all-reduce.6.cloned.1.call-update) | async-done | bytes 3145744 | tf_op jit(solution)/shard_map/psum | solution.py:116
  452.6 5.7 fusion.48
  459.1 3.9 multiply_reduce_fusion.3
  463.0 6.5 fusion.16
  472.2 10.4 %convert_reduce_fusion.1 = (f32[768]{0:T(1024)}, bf16[2048,768]{1,0:T(8,128)(2,1)S(1)}) fusion(f32[2048,768]{1,0:T(8,128)} %get-tuple-element.223, bf16[768,768]{1,0:T(8,128)(2,1)S(1)} %copy-done.45, f32[2048,768]{1,0:T(8,128)S(1)} %fusion.13, f32[2048,768]{1,0:T(8,128)} %get-tuple-element.242, f32[768]{0:T(1024)S(1)} %copy-done.43), kind=kOutput, calls=%fused_computation.45 | convolution fusion | flops 2444229888 | bytes 23205888 | tf_op jit(solution)/shard_map/td,fd->tf/dot_general | solution.py:134
  484.2 4.0 convolution_convert_fusion
  489.7 118.8 %all-reduce.8.cloned.1.call-done = bf16[2048,768]{1,0:T(8,128)(2,1)} async-done(((bf16[2048,768]{1,0:T(8,128)(2,1)}), bf16[2048,768]{1,0:T(8,128)(2,1)}) %all-reduce.8.cloned.1.call-update) | async-done | bytes 3145744 | tf_op jit(solution)/shard_map/psum | solution.py:143
  608.4 7.9 multiply_reduce_fusion.1
  616.8 5.7 fusion.52
  628.2 4.8 convolution_convert_fusion.3
  636.3 148.0 %while.25 = (s32[]{:T(128)}, f32[2,3072,192]{1,2,0:T(8,128)}, bf16[4,512,192]{1,2,0:T(8,128)(2,1)}, s32[4]{0:T(128)S(1)}, bf16[3,2048,192]{1,2,0:T(8,128)(2,1)},...) while((s32[]{:T(128)}, f32[2,3072,192]{1,2,0:T(8,128)}, ...), condition=%wide.region_19.20_spmd, body=%wide.region_17.19_spmd.sunk | while | flops 1533639168 | bytes 149576176 | solution.py:195
  648.1 5.6 multiply_reduce_fusion.7
  653.6 9.4 multiply_convert_fusion.3
  663.1 4.2 convolution_multiply_fusion.5
  669.9 3.5 fusion.116
  685.1 5.6 multiply_reduce_fusion.7
  690.8 9.5 multiply_convert_fusion.3
  700.2 4.2 convolution_multiply_fusion.5
  707.0 3.5 fusion.116
  722.2 5.5 multiply_reduce_fusion.7
  727.8 9.4 multiply_convert_fusion.3
  737.2 4.2 convolution_multiply_fusion.5
  743.9 3.5 fusion.116
  759.2 5.5 multiply_reduce_fusion.7
  764.7 9.4 multiply_convert_fusion.3
  774.1 4.2 convolution_multiply_fusion.5
  780.9 3.5 fusion.116
  788.8 5.2 fusion.24
  794.0 2.8 copy.48
  797.0 4.0 bitcast_convert_fusion
  801.2 8.2 fusion.38
  809.5 8.6 fusion.44
  821.6 14.6 %all-reduce.2 = (f32[2,192]{1,0:T(2,128)}, f32[768]{0:T(1024)}) all-reduce(f32[2,192]{1,0:T(2,128)S(1)} %pad_maximum_fusion.3, f32[768]{0:T(1024)S(1)} %copy-done.41), channel_id=1, replica_groups=mesh['dp'=8,'tensor'=4] {'dp'}, use_global_device_ids=true, to_apply=%region_23.24 | all-reduce | flops 1152 | bytes 9216 | tf_op jit(solution)/shard_map/psum | solution.py:211
  844.6 54.5 %reduce-scatter.11.cloned.1.call-done = bf16[512,768]{1,0:T(8,128)(2,1)} async-done(((bf16[2048,768]{1,0:T(8,128)(2,1)}), bf16[512,768]{1,0:T(8,128)(2,1)}) %reduce-scatter.11.cloned.1.call-update) | async-done | bytes 786448 | tf_op jit(solution)/shard_map/reduce_scatter | solution.py:207
  901.7 43.6 %reduce-scatter.17.cloned.1.call-done = f32[96,768]{1,0:T(8,128)} async-done(((f32[768,768]{1,0:T(8,128)}), f32[96,768]{1,0:T(8,128)}) %reduce-scatter.17.cloned.1.call-update) | async-done | bytes 294928 | tf_op jit(solution)/shard_map/reduce_scatter | solution.py:230
  945.2 46.3 %reduce-scatter.15.cloned.1.call-done = f32[96,768]{1,0:T(8,128)} async-done(((f32[768,768]{1,0:T(8,128)}), f32[96,768]{1,0:T(8,128)}) %reduce-scatter.15.cloned.1.call-update) | async-done | bytes 294928 | tf_op jit(solution)/shard_map/reduce_scatter | solution.py:229
  (307 shorter events, 136.2 us)
Async XLA Ops:
  7.2 301.7 %copy-start = (bf16[768,768]{1,0:T(8,128)(2,1)S(1)}, bf16[768,768]{1,0:T(8,128)(2,1)}, u32[]{:S(2)}) copy-start(bf16[768,768]{1,0:T(8,128)(2,1)} %param.27) | copy-start | bytes 3538948
  7.2 286.2 %all-gather.3.cloned.1.call-start = ((), (), s32[]{:S(2)}) async-start(), calls=%async_computation.12 | async-start | bytes 15728640 | tf_op jit(solution)/shard_map/all_gather | solution.py:100
  72.4 380.2 %all-reduce.6.cloned.1.call-start = ((), (), s32[]{:S(2)}) async-start(), calls=%async_computation.6 | async-start | bytes 6291456 | tf_op jit(solution)/shard_map/psum | solution.py:116
  73.3 543.1 %copy-start.33 = (f32[768]{0:T(1024)}, f32[768]{0:T(1024)S(1)}, u32[]{:S(2)}) copy-start(f32[768]{0:T(1024)S(1)} %convert_element_type.134) | copy-start | bytes 9220
  302.4 6.5 copy-start.34
  302.4 6.5 copy-start.38
  302.4 6.5 copy-start.42
  307.1 20.5 %copy-start.25 = (f32[2048]{0:T(1024)}, f32[2048]{0:T(1024)S(1)}, u32[]{:S(2)}) copy-start(f32[2048]{0:T(1024)S(1)} %broadcast_multiply_fusion.5) | copy-start | bytes 24580
  308.9 18.6 %copy-start.29 = (f32[2048]{0:T(1024)}, f32[2048]{0:T(1024)S(1)}, u32[]{:S(2)}) copy-start(f32[2048]{0:T(1024)S(1)} %add_rsqrt_fusion.1) | copy-start | bytes 24580
  308.9 20.2 %copy-start.44 = (bf16[768,768]{1,0:T(8,128)(2,1)S(1)}, bf16[768,768]{1,0:T(8,128)(2,1)}, u32[]{:S(2)}) copy-start(bf16[768,768]{1,0:T(8,128)(2,1)} %param.29) | copy-start | bytes 3538948
  333.2 275.3 %all-reduce.8.cloned.1.call-start = ((), (), s32[]{:S(2)}) async-start(), calls=%async_computation.7 | async-start | bytes 6291456 | tf_op jit(solution)/shard_map/psum | solution.py:143
  452.6 5.8 copy-start.8
  452.6 6.5 copy-start.15
  452.6 6.5 copy-start.26
  452.6 6.5 copy-start.30
  452.6 6.5 copy-start.35
  452.6 6.5 copy-start.39
  452.6 6.5 copy-start.40
  472.2 10.4 %copy-start.10 = (f32[2048,768]{1,0:T(8,128)}, f32[2048,768]{1,0:T(8,128)S(1)}, u32[]{:S(2)}) copy-start(f32[2048,768]{1,0:T(8,128)S(1)} %fusion.13) | copy-start | bytes 18874372
  488.2 348.0 %reduce-scatter.21.cloned.1.call-start = ((), (), s32[]{:S(2)}) async-start(), calls=%async_computation.14 | async-start | bytes 442368
  489.7 126.7 %copy-start.27 = (f32[2048]{0:T(1024)S(1)}, f32[2048]{0:T(1024)}, u32[]{:S(2)}) copy-start(f32[2048]{0:T(1024)} %copy-done.25) | copy-start | bytes 24580
  489.7 126.7 %copy-start.31 = (f32[2048]{0:T(1024)S(1)}, f32[2048]{0:T(1024)}, u32[]{:S(2)}) copy-start(f32[2048]{0:T(1024)} %copy-done.29) | copy-start | bytes 24580
  489.7 126.8 %copy-start.36 = (f32[768]{0:T(1024)S(1)}, f32[768]{0:T(1024)}, u32[]{:S(2)}) copy-start(f32[768]{0:T(1024)} %convert_element_type.135) | copy-start | bytes 9220
  608.4 8.0 copy-start.6
  608.4 8.0 copy-start.9
  608.4 8.3 copy-start.18
  616.8 8.4 copy-start.20
  628.1 212.8 %reduce-scatter.13.cloned.1.call-start = ((), (), s32[]{:S(2)}) async-start(), calls=%async_computation.9 | async-start | bytes 884736 | tf_op jit(solution)/shard_map/reduce_scatter | solution.py:227
  633.1 209.5 %reduce-scatter.19.cloned.1.call-start = ((), (), s32[]{:S(2)}) async-start(), calls=%async_computation.13 | async-start | bytes 2211840
  636.3 10.8 %copy-start.23 = (s32[3072]{0:T(1024)}, s32[3072]{0:T(1024)S(1)}, u32[]{:S(2)}) copy-start(s32[3072]{0:T(1024)S(1)} %get-tuple-element.459) | copy-start | bytes 36868 | tf_op jit(solution)/shard_map/while
  647.1 6.5 copy-start.2
  667.3 6.1 copy-start.24
  673.4 10.8 %copy-start.23 = (s32[3072]{0:T(1024)}, s32[3072]{0:T(1024)S(1)}, u32[]{:S(2)}) copy-start(s32[3072]{0:T(1024)S(1)} %get-tuple-element.459) | copy-start | bytes 36868 | tf_op jit(solution)/shard_map/while
  684.2 6.6 copy-start.2
  704.4 6.0 copy-start.24
  710.5 10.8 %copy-start.23 = (s32[3072]{0:T(1024)}, s32[3072]{0:T(1024)S(1)}, u32[]{:S(2)}) copy-start(s32[3072]{0:T(1024)S(1)} %get-tuple-element.459) | copy-start | bytes 36868 | tf_op jit(solution)/shard_map/while
  721.3 6.5 copy-start.2
  741.4 6.0 copy-start.24
  747.4 10.8 %copy-start.23 = (s32[3072]{0:T(1024)}, s32[3072]{0:T(1024)S(1)}, u32[]{:S(2)}) copy-start(s32[3072]{0:T(1024)S(1)} %get-tuple-element.459) | copy-start | bytes 36868 | tf_op jit(solution)/shard_map/while
  758.2 6.5 copy-start.2
  778.3 6.0 copy-start.24
  788.8 8.2 copy-start.46
  796.8 102.2 %reduce-scatter.11.cloned.1.call-start = ((), (), s32[]{:S(2)}) async-start(), calls=%async_computation.8 | async-start | bytes 3932160 | tf_op jit(solution)/shard_map/reduce_scatter | solution.py:207
  801.1 8.3 copy-start.28
  801.1 8.3 copy-start.32
  801.1 144.1 %reduce-scatter.17.cloned.1.call-start = ((), (), s32[]{:S(2)}) async-start(), calls=%async_computation.11 | async-start | bytes 2654208 | tf_op jit(solution)/shard_map/reduce_scatter | solution.py:230
  809.4 182.2 %reduce-scatter.15.cloned.1.call-start = ((), (), s32[]{:S(2)}) async-start(), calls=%async_computation.10 | async-start | bytes 2654208 | tf_op jit(solution)/shard_map/reduce_scatter | solution.py:229
  809.5 182.1 %copy-start.1 = (bf16[768,768]{1,0:T(8,128)(2,1)S(1)}, bf16[768,768]{1,0:T(8,128)(2,1)}, u32[]{:S(2)}) copy-start(bf16[768,768]{1,0:T(8,128)(2,1)} %param.27) | copy-start | bytes 3538948
  (27 other events, 72.1 us)
Sparse Core Ops, SparseCore 0:
  72.5 220.9 all-gather.2
  333.3 119.2 all-reduce.5
  488.4 120.0 all-reduce.7
  628.3 32.8 reduce-scatter.20
  664.2 34.9 reduce-scatter.12
  796.9 39.3 reduce-scatter.18
  838.6 60.4 reduce-scatter.10
  903.0 42.2 reduce-scatter.16
  949.2 42.3 reduce-scatter.14
